TPU v7x, 32 devices: a whole 2x2x4 slice. The times are simulated.
32 devices in a mesh: dp: 8 (over z, x), space: 4 (over y, core).
Axes of the slice: x: 2, y: 2, z: 4, core: 2. Of those that a mesh axis runs over, the one named last changes fastest.
Arguments:
- latents: bfloat16 [48, 8, 32, 1280], P('dp', 'space'), may hold values from -42 to 42
- buckets: int32 [48, 2], P('dp'), may hold values from 6 to 32, as said below
- gn_gain: float32 [1280], replicated, may hold values from 0.1 to 1.9
- gn_shift: float32 [1280], replicated, may hold values from -3 to 3
- conv_weight: bfloat16 [9, 1280, 1280], P(None, 'dp'), may hold values from -0.0546875 to 0.0546875
- time_bias: float32 [48, 1280], P('dp'), may hold values from -5 to 5
Outputs:
- result: bfloat16 [48, 8, 32, 1280], P('dp', 'space')
Inputs may be any that keep to these rules, and one draw needn't show every extreme that they name: `buckets`: column 0 is a frame's height, column 1 its width; heights are at least 6 and at most 8, widths at least 24 and at most 32; in every draw some frame has height 8 and width 32.
All inputs are finite; a program needn't handle non-finite values.
Results may differ from a plain program's by a relative error of at most 0.0035.
Values may be sent and summed in bfloat16 or wider, within the bound.
No kernel may reach another device: no remote copies, remote signals or barrier semaphores. Data moves between devices by JAX's collectives and lax.ppermute only.
A program may use at most 64 MiB of HBM per device.

v0:
```python
import jax
import jax.numpy as jnp
from jax import lax
from jax.sharding import PartitionSpec as P

GROUPS = 32
eps = 1e-05


def with_halo(x, sides, width):
    for axis, dim in sides:
        size, length = (lax.axis_size(axis), x.shape[dim])
        up = [(i, (i + 1) % size) for i in range(size - 1)]
        down = [(j, i) for i, j in up]
        last = lax.slice_in_dim(x, length - width, length, axis=dim)
        first = lax.slice_in_dim(x, 0, width, axis=dim)
        before = lax.ppermute(last, axis, up)
        after = lax.ppermute(first, axis, down)
        x = jnp.concatenate([before, x, after], axis=dim)
    return x


def tap_product(window, panel):
    return lax.dot_general(
        window, panel, (((3,), (1,)), ((), ())), preferred_element_type=jnp.float32
    )


def on_device(latents, buckets, gn_gain, gn_shift, conv_weight, time_bias):
    frames, rows, cols, chans = latents.shape
    members = chans // GROUPS
    row_ids = lax.axis_index("space") * rows + jnp.arange(rows, dtype=jnp.int32)
    col_ids = jnp.arange(cols, dtype=jnp.int32)
    valid = (
        (row_ids[None, :, None] < buckets[:, 0][:, None, None])
        & (col_ids[None, None, :] < buckets[:, 1][:, None, None])
    ).astype(jnp.float32)
    count = (buckets[:, 0] * buckets[:, 1]).astype(jnp.float32)[:, None] * members
    values = latents.astype(jnp.float32).reshape(frames, rows, cols, GROUPS, members)
    weight_mask = valid[:, :, :, None, None]
    total = lax.psum(jnp.sum(values * weight_mask, axis=(1, 2, 4)), "space")
    mean = total / count
    centered = values - mean[:, None, None, :, None]
    spread = lax.psum(jnp.sum(centered * centered * weight_mask, axis=(1, 2, 4)), "space") / count
    normed = (centered / jnp.sqrt(spread[:, None, None, :, None] + eps)).reshape(
        frames, rows, cols, chans
    )
    normed = normed * gn_gain + gn_shift
    act = (valid[..., None] * jax.nn.silu(normed)).astype(jnp.bfloat16)
    extended = with_halo(act, (("space", 1),), 1)
    padded = jnp.pad(extended, ((0, 0), (0, 0), (1, 1), (0, 0)))

    def add_tap(index, accum):
        window = lax.dynamic_slice(
            padded, (0, index // 3, index % 3, 0), (frames, rows, cols, chans)
        )
        panel = lax.dynamic_index_in_dim(conv_weight, index, 0, keepdims=False)
        return accum + tap_product(window, lax.all_gather(panel, "dp", axis=0, tiled=True))

    conv = lax.fori_loop(0, 9, add_tap, jnp.zeros((frames, rows, cols, chans), jnp.float32))
    conv_out = conv.astype(jnp.bfloat16)
    summed = latents.astype(jnp.float32) + valid[..., None] * (
        conv_out.astype(jnp.float32) + time_bias[:, None, None, :]
    )
    return summed.astype(jnp.bfloat16)


def solution(mesh):
    in_specs = (
        P("dp", "space", None, None),
        P("dp", None),
        P(),
        P(),
        P(None, "dp", None),
        P("dp", None),
    )
    out_specs = P("dp", "space", None, None)
    return jax.shard_map(
        on_device, mesh=mesh, in_specs=in_specs, out_specs=out_specs, check_vma=False
    )
```

profile of v0, /device:TPU:0, one launch (start us, length us, event | category | flops | bytes accessed | tf_op | source)
XLA Modules:
  0.0 674.8 jit_solution(2371292868569001316)
XLA Ops:
  6.5 0.8 multiply_bitcast_fusion
  7.3 0.8 slice_bitcast_fusion.1
  8.3 1.6 fusion.19
  9.9 0.1 reduce_sum.24
  10.0 0.1 reduce_sum.25
  10.1 8.4 %psum.14 = f32[6,32]{1,0:T(8,128)S(1)} all-reduce(f32[6,32]{1,0:T(8,128)S(1)} %reduce_sum.25), channel_id=1, replica_groups=mesh['dp'=8,'space'=4] {'space'}, use_global_device_ids=true, to_apply=%region_2.0 | all-reduce | flops 192 | bytes 1536 | tf_op jit(solution)/shard_map/psum | solution.py:41
  18.6 0.1 sub.21
  18.8 0.5 fusion.16
  19.3 0.1 reduce_sum.36
  19.4 0.1 reduce_sum.37
  19.5 5.8 psum.15
  25.4 0.1 div.49
  25.6 0.8 multiply_convert_fusion
  26.4 0.8 fusion.21
  27.2 1.7 collective-permute-start
  28.9 1.3 collective-permute-start.1
  30.2 0.3 collective-permute-done
  30.6 2.2 collective-permute-done.1
  32.8 1.9 fusion.12
  34.7 630.7 %while.16 = (s32[]{:T(128)}, f32[6,2,32,1280]{3,2,1,0:T(8,128)}, bf16[6,4,34,1280]{3,2,1,0:T(8,128)(2,1)}, bf16[9,160,1280]{2,1,0:T(8,128)(2,1)}, s32[]{:T(128)}...) while((s32[]{:T(128)}, f32[6,2,32,1280]{3,2,1,0:T(8,128)}, ...), condition=%wide.region_7.8_spmd.clone, body=%wide.region_6.7_spmd.clone.sunk | while | flops 1259274240 | bytes 20070744 | solution.py:60
  34.7 1.8 constant_dynamic-slice_fusion.2
  36.6 70.1 %all-gather.6.cloned.1.call-done = bf16[1,1280,1280]{2,1,0:T(8,128)(2,1)} async-done(((bf16[1,160,1280]{2,1,0:T(8,128)(2,1)}), bf16[1,1280,1280]{2,1,0:T(8,128)(2,1)}) %all-gather.6.cloned.1.call-update) | async-done | bytes 3276816 | tf_op jit(solution)/shard_map/while/body/eval_jaxpr/all_gather | solution.py:58
  106.7 5.1 fusion.27
  111.8 1.8 constant_dynamic-slice_fusion.2
  113.6 61.7 %all-gather.6.cloned.1.call-done = bf16[1,1280,1280]{2,1,0:T(8,128)(2,1)} async-done(((bf16[1,160,1280]{2,1,0:T(8,128)(2,1)}), bf16[1,1280,1280]{2,1,0:T(8,128)(2,1)}) %all-gather.6.cloned.1.call-update) | async-done | bytes 3276816 | tf_op jit(solution)/shard_map/while/body/eval_jaxpr/all_gather | solution.py:58
  175.4 5.7 fusion.27
  181.1 1.8 constant_dynamic-slice_fusion.2
  182.9 61.7 %all-gather.6.cloned.1.call-done = bf16[1,1280,1280]{2,1,0:T(8,128)(2,1)} async-done(((bf16[1,160,1280]{2,1,0:T(8,128)(2,1)}), bf16[1,1280,1280]{2,1,0:T(8,128)(2,1)}) %all-gather.6.cloned.1.call-update) | async-done | bytes 3276816 | tf_op jit(solution)/shard_map/while/body/eval_jaxpr/all_gather | solution.py:58
  244.7 5.7 fusion.27
  250.4 1.8 constant_dynamic-slice_fusion.2
  252.2 61.4 %all-gather.6.cloned.1.call-done = bf16[1,1280,1280]{2,1,0:T(8,128)(2,1)} async-done(((bf16[1,160,1280]{2,1,0:T(8,128)(2,1)}), bf16[1,1280,1280]{2,1,0:T(8,128)(2,1)}) %all-gather.6.cloned.1.call-update) | async-done | bytes 3276816 | tf_op jit(solution)/shard_map/while/body/eval_jaxpr/all_gather | solution.py:58
  313.7 5.7 fusion.27
  319.4 1.8 constant_dynamic-slice_fusion.2
  321.3 61.4 %all-gather.6.cloned.1.call-done = bf16[1,1280,1280]{2,1,0:T(8,128)(2,1)} async-done(((bf16[1,160,1280]{2,1,0:T(8,128)(2,1)}), bf16[1,1280,1280]{2,1,0:T(8,128)(2,1)}) %all-gather.6.cloned.1.call-update) | async-done | bytes 3276816 | tf_op jit(solution)/shard_map/while/body/eval_jaxpr/all_gather | solution.py:58
  382.7 5.7 fusion.27
  388.4 1.8 constant_dynamic-slice_fusion.2
  390.3 61.4 %all-gather.6.cloned.1.call-done = bf16[1,1280,1280]{2,1,0:T(8,128)(2,1)} async-done(((bf16[1,160,1280]{2,1,0:T(8,128)(2,1)}), bf16[1,1280,1280]{2,1,0:T(8,128)(2,1)}) %all-gather.6.cloned.1.call-update) | async-done | bytes 3276816 | tf_op jit(solution)/shard_map/while/body/eval_jaxpr/all_gather | solution.py:58
  451.7 5.7 fusion.27
  457.4 1.8 constant_dynamic-slice_fusion.2
  459.3 61.8 %all-gather.6.cloned.1.call-done = bf16[1,1280,1280]{2,1,0:T(8,128)(2,1)} async-done(((bf16[1,160,1280]{2,1,0:T(8,128)(2,1)}), bf16[1,1280,1280]{2,1,0:T(8,128)(2,1)}) %all-gather.6.cloned.1.call-update) | async-done | bytes 3276816 | tf_op jit(solution)/shard_map/while/body/eval_jaxpr/all_gather | solution.py:58
  521.0 5.7 fusion.27
  526.7 1.8 constant_dynamic-slice_fusion.2
  528.6 61.8 %all-gather.6.cloned.1.call-done = bf16[1,1280,1280]{2,1,0:T(8,128)(2,1)} async-done(((bf16[1,160,1280]{2,1,0:T(8,128)(2,1)}), bf16[1,1280,1280]{2,1,0:T(8,128)(2,1)}) %all-gather.6.cloned.1.call-update) | async-done | bytes 3276816 | tf_op jit(solution)/shard_map/while/body/eval_jaxpr/all_gather | solution.py:58
  590.3 5.7 fusion.27
  596.1 1.8 constant_dynamic-slice_fusion.2
  597.9 61.7 %all-gather.6.cloned.1.call-done = bf16[1,1280,1280]{2,1,0:T(8,128)(2,1)} async-done(((bf16[1,160,1280]{2,1,0:T(8,128)(2,1)}), bf16[1,1280,1280]{2,1,0:T(8,128)(2,1)}) %all-gather.6.cloned.1.call-update) | async-done | bytes 3276816 | tf_op jit(solution)/shard_map/while/body/eval_jaxpr/all_gather | solution.py:58
  659.7 5.7 fusion.27
  665.4 2.9 fusion.20
  (35 shorter events, 0.7 us)
Async XLA Ops:
  6.5 12.2 %copy-start = (bf16[6,2,32,1280]{3,2,1,0:T(8,128)(2,1)S(1)}, bf16[6,2,32,1280]{3,2,1,0:T(8,128)(2,1)}, u32[]{:S(2)}) copy-start(bf16[6,2,32,1280]{3,2,1,0:T(8,128)(2,1)} %param.8) | copy-start | bytes 2949124
  6.5 19.0 %copy-start.2 = (f32[1280]{0:T(1024)S(1)}, f32[1280]{0:T(1024)}, u32[]{:S(2)}) copy-start(f32[1280]{0:T(1024)} %param.11) | copy-start | bytes 15364
  6.5 19.0 %copy-start.3 = (f32[1280]{0:T(1024)S(1)}, f32[1280]{0:T(1024)}, u32[]{:S(2)}) copy-start(f32[1280]{0:T(1024)} %param.10) | copy-start | bytes 15364
  27.2 3.3 collective-permute-start
  28.9 3.9 collective-permute-start.1
  34.7 630.7 %copy-start.1 = (f32[6,1280]{1,0:T(8,128)S(1)}, f32[6,1280]{1,0:T(8,128)}, u32[]{:S(2)}) copy-start(f32[6,1280]{1,0:T(8,128)} %param.13) | copy-start | bytes 92164
  34.7 71.9 %all-gather.6.cloned.1.call-start = ((), (), s32[]{:S(2)}) async-start(), calls=%async_computation | async-start | bytes 3686400 | tf_op jit(solution)/shard_map/while/body/eval_jaxpr/all_gather | solution.py:58
  111.8 63.6 %all-gather.6.cloned.1.call-start = ((), (), s32[]{:S(2)}) async-start(), calls=%async_computation | async-start | bytes 3686400 | tf_op jit(solution)/shard_map/while/body/eval_jaxpr/all_gather | solution.py:58
  181.1 63.6 %all-gather.6.cloned.1.call-start = ((), (), s32[]{:S(2)}) async-start(), calls=%async_computation | async-start | bytes 3686400 | tf_op jit(solution)/shard_map/while/body/eval_jaxpr/all_gather | solution.py:58
  250.4 63.3 %all-gather.6.cloned.1.call-start = ((), (), s32[]{:S(2)}) async-start(), calls=%async_computation | async-start | bytes 3686400 | tf_op jit(solution)/shard_map/while/body/eval_jaxpr/all_gather | solution.py:58
  319.4 63.3 %all-gather.6.cloned.1.call-start = ((), (), s32[]{:S(2)}) async-start(), calls=%async_computation | async-start | bytes 3686400 | tf_op jit(solution)/shard_map/while/body/eval_jaxpr/all_gather | solution.py:58
  388.4 63.3 %all-gather.6.cloned.1.call-start = ((), (), s32[]{:S(2)}) async-start(), calls=%async_computation | async-start | bytes 3686400 | tf_op jit(solution)/shard_map/while/body/eval_jaxpr/all_gather | solution.py:58
  457.4 63.6 %all-gather.6.cloned.1.call-start = ((), (), s32[]{:S(2)}) async-start(), calls=%async_computation | async-start | bytes 3686400 | tf_op jit(solution)/shard_map/while/body/eval_jaxpr/all_gather | solution.py:58
  526.7 63.6 %all-gather.6.cloned.1.call-start = ((), (), s32[]{:S(2)}) async-start(), calls=%async_computation | async-start | bytes 3686400 | tf_op jit(solution)/shard_map/while/body/eval_jaxpr/all_gather | solution.py:58
  596.1 63.6 %all-gather.6.cloned.1.call-start = ((), (), s32[]{:S(2)}) async-start(), calls=%async_computation | async-start | bytes 3686400 | tf_op jit(solution)/shard_map/while/body/eval_jaxpr/all_gather | solution.py:58
Sparse Core Ops, SparseCore 0:
  37.7 68.8 all-gather.5
  114.8 60.5 all-gather.5
  184.1 60.5 all-gather.5
  253.1 60.5 all-gather.5
  322.1 60.5 all-gather.5
  391.1 60.5 all-gather.5
  460.4 60.5 all-gather.5
  529.8 60.5 all-gather.5
  599.1 60.5 all-gather.5
where the time goes:
time: 675 us
  waiting for transfers between devices  566 us (84%)
  matrix products  50.9 us (8%)
  local copies, waits for them, and re-layouts  18.2 us (3%)
  blocking collectives  14.1 us (2%)
  between operations  13.2 us (2%)
  other arithmetic  9.07 us (1%)
    all_gather x9, waiting for transfers between devices, add_tap(): lax.all_gather(panel, 'dp', axis=0, tiled=True)  563 us
    dot_general x9, matrix products, tap_product(): lax.dot_general(window, panel, (((3,), (1,)), ((), ())), preferred_elemen...  50.9 us
    dynamic_slice x9, local copies, waits for them, and re-layouts, add_tap(): panel = lax.dynamic_index_in_dim(conv_weight, index, 0, keepdims=False)  16 us
  transfers between devices with their start and end apart: 11, of which 11 were waited for; matrix products, arithmetic and copies ran while one was open for 0% of the time, Pallas kernels for 0%

commit v1 on v0

--- a/solution.py
+++ b/solution.py
@@ -5,6 +5,24 @@
 
 GROUPS = 32
 eps = 1e-05
+
+
+def ring_gather(value, axis, dim):
+    ways, here, hop = (lax.axis_size(axis), lax.axis_index(axis), value.shape[dim])
+    shape = [n * ways if d == dim else n for d, n in enumerate(value.shape)]
+    full = lax.dynamic_update_slice_in_dim(
+        jnp.zeros(shape, value.dtype), value, here * hop, axis=dim
+    )
+    going_up = going_down = value
+    for far in range(1, ways // 2 + 1):
+        going_up = lax.ppermute(going_up, axis, [(d, (d + 1) % ways) for d in range(ways)])
+        full = lax.dynamic_update_slice_in_dim(full, going_up, (here - far) % ways * hop, axis=dim)
+        if 2 * far < ways:
+            going_down = lax.ppermute(going_down, axis, [(d, (d - 1) % ways) for d in range(ways)])
+            full = lax.dynamic_update_slice_in_dim(
+                full, going_down, (here + far) % ways * hop, axis=dim
+            )
+    return full
 
 
 def with_halo(x, sides, width):
@@ -55,7 +73,7 @@
             padded, (0, index // 3, index % 3, 0), (frames, rows, cols, chans)
         )
         panel = lax.dynamic_index_in_dim(conv_weight, index, 0, keepdims=False)
-        return accum + tap_product(window, lax.all_gather(panel, "dp", axis=0, tiled=True))
+        return accum + tap_product(window, ring_gather(panel, "dp", 0))
 
     conv = lax.fori_loop(0, 9, add_tap, jnp.zeros((frames, rows, cols, chans), jnp.float32))
     conv_out = conv.astype(jnp.bfloat16)

time: 675 us -> 703 us (1.041)
  starting transfers between devices: 3 us -> 200 us
  waiting for transfers between devices: 566 us -> 394 us
  local copies, waits for them, and re-layouts: 18.2 us -> 52.5 us
  matrix products: 50.9 us -> 29.8 us
  between operations: 13.2 us -> 0.14 us
    all_gather x9 -> x0, waiting for transfers between devices: 563 us -> none  [add_tap(): lax.all_gather(panel, 'dp', axis=0, tiled=True)]
    ppermute x0 -> x63, waiting for transfers between devices: none -> 392 us  [the longest x36 385 us: ring_gather(): lax.ppermute(going_up, axis, [(d, (d + 1) % ways) for d in range(ways)])]
    ppermute x0 -> x63, starting transfers between devices: none -> 197 us  [the longest x27 129 us: ring_gather(): lax.ppermute(going_down, axis, [(d, (d - 1) % ways) for d in range(ways)])]
    dynamic_update_slice x0 -> x72, local copies, waits for them, and re-layouts: none -> 37.6 us  [the longest x9 16.3 us: ring_gather(): lax.dynamic_update_slice_in_dim(jnp.zeros(shape, value.dtype), value, her...]
    dot_general x9, matrix products: 50.9 us -> 29.8 us  [tap_product(): lax.dot_general(window, panel, (((3,), (1,)), ((), ())), preferred_elemen...]
    dynamic_slice x9 -> x0, local copies, waits for them, and re-layouts: 16 us -> none  [add_tap(): panel = lax.dynamic_index_in_dim(conv_weight, index, 0, keepdims=False)]
    while x0 -> x36, local copies, waits for them, and re-layouts: none -> 11.5 us
  transfers between devices with their start and end apart: 11 -> 65, of which waited for: 11 -> 46; matrix products, arithmetic and copies ran while one was open for 0% -> 3% of each run, Pallas kernels for 0% -> 0%
where the time goes in v1:
time: 703 us; the launch traced here: 702 us
  waiting for transfers between devices  394 us (56%)
  starting transfers between devices  200 us (28%)
  local copies, waits for them, and re-layouts  52.5 us (7%)
  matrix products  29.8 us (4%)
  blocking collectives  14.2 us (2%)
  other arithmetic  10.5 us (1%)
    ppermute x36, waiting for transfers between devices, ring_gather(): lax.ppermute(going_up, axis, [(d, (d + 1) % ways) for d in range(ways)])  385 us
    ppermute x27, starting transfers between devices, ring_gather(): lax.ppermute(going_down, axis, [(d, (d - 1) % ways) for d in range(ways)])  129 us
    ppermute x36, starting transfers between devices, ring_gather(): lax.ppermute(going_up, axis, [(d, (d + 1) % ways) for d in range(ways)])  67.7 us
    dot_general x9, matrix products, tap_product(): lax.dot_general(window, panel, (((3,), (1,)), ((), ())), preferred_elemen...  29.8 us
    dynamic_update_slice x9, local copies, waits for them, and re-layouts, ring_gather(): lax.dynamic_update_slice_in_dim(jnp.zeros(shape, value.dtype), value, her...  16.3 us
  transfers between devices with their start and end apart: 65, of which 46 were waited for; matrix products, arithmetic and copies ran while one was open for 3% of the time, Pallas kernels for 0%

profile of v1, /device:TPU:0, one launch (start us, length us, event | category | flops | bytes accessed | tf_op | source)
XLA Modules:
  0.0 701.5 jit_solution(13000951304614980459)
XLA Ops:
  3.6 8.4 %psum.14 = f32[6,32]{1,0:T(8,128)S(1)} all-reduce(f32[6,32]{1,0:T(8,128)S(1)} %reduce_sum.25), channel_id=1, replica_groups=mesh['dp'=8,'space'=4] {'space'}, use_global_device_ids=true, to_apply=%region_2.0 | all-reduce | flops 192 | bytes 1536 | tf_op jit(solution)/shard_map/psum | solution.py:59
  14.1 5.8 psum.15
  28.6 669.7 %while.17 = (s32[]{:T(128)}, f32[6,2,32,1280]{3,2,1,0:T(8,128)}, bf16[6,4,34,1280]{3,2,1,0:T(8,128)(2,1)}, bf16[9,160,1280]{2,1,0:T(8,128)(2,1)}, s32[]{:T(128)}...) while((s32[]{:T(128)}, f32[6,2,32,1280]{3,2,1,0:T(8,128)}, ...), condition=%wide.region_7.8_spmd.clone, body=%wide.region_6.7_spmd.clone.sunk | while | flops 1259274368 | bytes 45631428 | solution.py:78
  35.3 13.2 %collective-permute-done = bf16[160,1280]{1,0:T(8,128)(2,1)} collective-permute-done((bf16[160,1280]{1,0:T(8,128)(2,1)}, bf16[160,1280]{1,0:T(8,128)(2,1)}, u32[]{:S(2)}, u32[]{:S(2)}) %collective-permute-start) | collective-permute-done | bytes 409632 | tf_op jit(solution)/shard_map/while/body/eval_jaxpr/ppermute | solution.py:18
  56.2 12.3 %collective-permute-done.2 = bf16[160,1280]{1,0:T(8,128)(2,1)S(1)} collective-permute-done((bf16[160,1280]{1,0:T(8,128)(2,1)}, bf16[160,1280]{1,0:T(8,128)(2,1)S(1)}, u32[]{:S(2)}, u32[]{:S(2)}) %collective-permute-start.2) | collective-permute-done | bytes 409632 | tf_op jit(solution)/shard_map/while/body/eval_jaxpr/ppermute | solution.py:18
  73.3 15.9 %collective-permute-done.4 = bf16[160,1280]{1,0:T(8,128)(2,1)S(1)} collective-permute-done((bf16[160,1280]{1,0:T(8,128)(2,1)S(1)}, bf16[160,1280]{1,0:T(8,128)(2,1)S(1)}, u32[]{:S(2)}, u32[]{:S(2)}) %collective-permute-start.4) | collective-permute-done | bytes 409632 | tf_op jit(solution)/shard_map/while/body/eval_jaxpr/ppermute | solution.py:18
  92.3 11.4 %collective-permute-done.6 = bf16[160,1280]{1,0:T(8,128)(2,1)S(1)} collective-permute-done((bf16[160,1280]{1,0:T(8,128)(2,1)S(1)}, bf16[160,1280]{1,0:T(8,128)(2,1)S(1)}, u32[]{:S(2)}, u32[]{:S(2)}) %collective-permute-start.6) | collective-permute-done | bytes 409632 | tf_op jit(solution)/shard_map/while/body/eval_jaxpr/ppermute | solution.py:18
  110.4 4.7 collective-permute-start.1
  115.2 13.3 %collective-permute-done = bf16[160,1280]{1,0:T(8,128)(2,1)} collective-permute-done((bf16[160,1280]{1,0:T(8,128)(2,1)}, bf16[160,1280]{1,0:T(8,128)(2,1)}, u32[]{:S(2)}, u32[]{:S(2)}) %collective-permute-start) | collective-permute-done | bytes 409632 | tf_op jit(solution)/shard_map/while/body/eval_jaxpr/ppermute | solution.py:18
  135.4 12.7 %collective-permute-done.2 = bf16[160,1280]{1,0:T(8,128)(2,1)S(1)} collective-permute-done((bf16[160,1280]{1,0:T(8,128)(2,1)}, bf16[160,1280]{1,0:T(8,128)(2,1)S(1)}, u32[]{:S(2)}, u32[]{:S(2)}) %collective-permute-start.2) | collective-permute-done | bytes 409632 | tf_op jit(solution)/shard_map/while/body/eval_jaxpr/ppermute | solution.py:18
  152.9 14.3 %collective-permute-done.4 = bf16[160,1280]{1,0:T(8,128)(2,1)S(1)} collective-permute-done((bf16[160,1280]{1,0:T(8,128)(2,1)S(1)}, bf16[160,1280]{1,0:T(8,128)(2,1)S(1)}, u32[]{:S(2)}, u32[]{:S(2)}) %collective-permute-start.4) | collective-permute-done | bytes 409632 | tf_op jit(solution)/shard_map/while/body/eval_jaxpr/ppermute | solution.py:18
  169.9 10.5 %collective-permute-done.6 = bf16[160,1280]{1,0:T(8,128)(2,1)S(1)} collective-permute-done((bf16[160,1280]{1,0:T(8,128)(2,1)S(1)}, bf16[160,1280]{1,0:T(8,128)(2,1)S(1)}, u32[]{:S(2)}, u32[]{:S(2)}) %collective-permute-start.6) | collective-permute-done | bytes 409632 | tf_op jit(solution)/shard_map/while/body/eval_jaxpr/ppermute | solution.py:18
  187.0 4.7 collective-permute-start.1
  191.7 11.7 %collective-permute-done = bf16[160,1280]{1,0:T(8,128)(2,1)} collective-permute-done((bf16[160,1280]{1,0:T(8,128)(2,1)}, bf16[160,1280]{1,0:T(8,128)(2,1)}, u32[]{:S(2)}, u32[]{:S(2)}) %collective-permute-start) | collective-permute-done | bytes 409632 | tf_op jit(solution)/shard_map/while/body/eval_jaxpr/ppermute | solution.py:18
  205.8 7.5 %collective-permute-start.3 = (bf16[160,1280]{1,0:T(8,128)(2,1)}, bf16[160,1280]{1,0:T(8,128)(2,1)S(1)}, u32[]{:S(2)}, u32[]{:S(2)}) collective-permute-start(bf16[160,1280]{1,0:T(8,128)(2,1)} %collective-permute-done.1), channel_id=1, source_target_pairs={{0,28},{4,0},{8,4},{12,8},{16,12},{20,16},{24,20},{28,24},{1,29},{... | collective-permute-start | bytes 1228808 | tf_op jit(solution)/shard_map/while/body/eval_jaxpr/ppermute | solution.py:21
  215.6 6.6 collective-permute-done.2
  224.6 9.2 %collective-permute-start.5 = (bf16[160,1280]{1,0:T(8,128)(2,1)S(1)}, bf16[160,1280]{1,0:T(8,128)(2,1)S(1)}, u32[]{:S(2)}, u32[]{:S(2)}) collective-permute-start(bf16[160,1280]{1,0:T(8,128)(2,1)S(1)} %collective-permute-done.3), channel_id=1, source_target_pairs={{0,28},{4,0},{8,4},{12,8},{16,12},{20,16},{24,20},{28,24},{1,29},{... | collective-permute-start | bytes 1228808 | tf_op jit(solution)/shard_map/while/body/eval_jaxpr/ppermute | solution.py:21
  233.9 7.4 %collective-permute-done.4 = bf16[160,1280]{1,0:T(8,128)(2,1)S(1)} collective-permute-done((bf16[160,1280]{1,0:T(8,128)(2,1)S(1)}, bf16[160,1280]{1,0:T(8,128)(2,1)S(1)}, u32[]{:S(2)}, u32[]{:S(2)}) %collective-permute-start.4) | collective-permute-done | bytes 409632 | tf_op jit(solution)/shard_map/while/body/eval_jaxpr/ppermute | solution.py:18
  243.9 10.5 %collective-permute-done.6 = bf16[160,1280]{1,0:T(8,128)(2,1)S(1)} collective-permute-done((bf16[160,1280]{1,0:T(8,128)(2,1)S(1)}, bf16[160,1280]{1,0:T(8,128)(2,1)S(1)}, u32[]{:S(2)}, u32[]{:S(2)}) %collective-permute-start.6) | collective-permute-done | bytes 409632 | tf_op jit(solution)/shard_map/while/body/eval_jaxpr/ppermute | solution.py:18
  265.8 11.7 %collective-permute-done = bf16[160,1280]{1,0:T(8,128)(2,1)} collective-permute-done((bf16[160,1280]{1,0:T(8,128)(2,1)}, bf16[160,1280]{1,0:T(8,128)(2,1)}, u32[]{:S(2)}, u32[]{:S(2)}) %collective-permute-start) | collective-permute-done | bytes 409632 | tf_op jit(solution)/shard_map/while/body/eval_jaxpr/ppermute | solution.py:18
  285.2 11.0 %collective-permute-done.2 = bf16[160,1280]{1,0:T(8,128)(2,1)S(1)} collective-permute-done((bf16[160,1280]{1,0:T(8,128)(2,1)}, bf16[160,1280]{1,0:T(8,128)(2,1)S(1)}, u32[]{:S(2)}, u32[]{:S(2)}) %collective-permute-start.2) | collective-permute-done | bytes 409632 | tf_op jit(solution)/shard_map/while/body/eval_jaxpr/ppermute | solution.py:18
  302.6 12.7 %collective-permute-done.4 = bf16[160,1280]{1,0:T(8,128)(2,1)S(1)} collective-permute-done((bf16[160,1280]{1,0:T(8,128)(2,1)S(1)}, bf16[160,1280]{1,0:T(8,128)(2,1)S(1)}, u32[]{:S(2)}, u32[]{:S(2)}) %collective-permute-start.4) | collective-permute-done | bytes 409632 | tf_op jit(solution)/shard_map/while/body/eval_jaxpr/ppermute | solution.py:18
  317.9 10.5 %collective-permute-done.6 = bf16[160,1280]{1,0:T(8,128)(2,1)S(1)} collective-permute-done((bf16[160,1280]{1,0:T(8,128)(2,1)S(1)}, bf16[160,1280]{1,0:T(8,128)(2,1)S(1)}, u32[]{:S(2)}, u32[]{:S(2)}) %collective-permute-start.6) | collective-permute-done | bytes 409632 | tf_op jit(solution)/shard_map/while/body/eval_jaxpr/ppermute | solution.py:18
  339.9 11.2 %collective-permute-done = bf16[160,1280]{1,0:T(8,128)(2,1)} collective-permute-done((bf16[160,1280]{1,0:T(8,128)(2,1)}, bf16[160,1280]{1,0:T(8,128)(2,1)}, u32[]{:S(2)}, u32[]{:S(2)}) %collective-permute-start) | collective-permute-done | bytes 409632 | tf_op jit(solution)/shard_map/while/body/eval_jaxpr/ppermute | solution.py:18
  358.7 10.6 %collective-permute-done.2 = bf16[160,1280]{1,0:T(8,128)(2,1)S(1)} collective-permute-done((bf16[160,1280]{1,0:T(8,128)(2,1)}, bf16[160,1280]{1,0:T(8,128)(2,1)S(1)}, u32[]{:S(2)}, u32[]{:S(2)}) %collective-permute-start.2) | collective-permute-done | bytes 409632 | tf_op jit(solution)/shard_map/while/body/eval_jaxpr/ppermute | solution.py:18
  374.9 13.5 %collective-permute-done.4 = bf16[160,1280]{1,0:T(8,128)(2,1)S(1)} collective-permute-done((bf16[160,1280]{1,0:T(8,128)(2,1)S(1)}, bf16[160,1280]{1,0:T(8,128)(2,1)S(1)}, u32[]{:S(2)}, u32[]{:S(2)}) %collective-permute-start.4) | collective-permute-done | bytes 409632 | tf_op jit(solution)/shard_map/while/body/eval_jaxpr/ppermute | solution.py:18
  391.1 10.4 %collective-permute-done.6 = bf16[160,1280]{1,0:T(8,128)(2,1)S(1)} collective-permute-done((bf16[160,1280]{1,0:T(8,128)(2,1)S(1)}, bf16[160,1280]{1,0:T(8,128)(2,1)S(1)}, u32[]{:S(2)}, u32[]{:S(2)}) %collective-permute-start.6) | collective-permute-done | bytes 409632 | tf_op jit(solution)/shard_map/while/body/eval_jaxpr/ppermute | solution.py:18
  412.9 11.6 %collective-permute-done = bf16[160,1280]{1,0:T(8,128)(2,1)} collective-permute-done((bf16[160,1280]{1,0:T(8,128)(2,1)}, bf16[160,1280]{1,0:T(8,128)(2,1)}, u32[]{:S(2)}, u32[]{:S(2)}) %collective-permute-start) | collective-permute-done | bytes 409632 | tf_op jit(solution)/shard_map/while/body/eval_jaxpr/ppermute | solution.py:18
  431.4 12.1 %collective-permute-done.2 = bf16[160,1280]{1,0:T(8,128)(2,1)S(1)} collective-permute-done((bf16[160,1280]{1,0:T(8,128)(2,1)}, bf16[160,1280]{1,0:T(8,128)(2,1)S(1)}, u32[]{:S(2)}, u32[]{:S(2)}) %collective-permute-start.2) | collective-permute-done | bytes 409632 | tf_op jit(solution)/shard_map/while/body/eval_jaxpr/ppermute | solution.py:18
  448.3 13.8 %collective-permute-done.4 = bf16[160,1280]{1,0:T(8,128)(2,1)S(1)} collective-permute-done((bf16[160,1280]{1,0:T(8,128)(2,1)S(1)}, bf16[160,1280]{1,0:T(8,128)(2,1)S(1)}, u32[]{:S(2)}, u32[]{:S(2)}) %collective-permute-start.4) | collective-permute-done | bytes 409632 | tf_op jit(solution)/shard_map/while/body/eval_jaxpr/ppermute | solution.py:18
  464.8 10.0 %collective-permute-done.6 = bf16[160,1280]{1,0:T(8,128)(2,1)S(1)} collective-permute-done((bf16[160,1280]{1,0:T(8,128)(2,1)S(1)}, bf16[160,1280]{1,0:T(8,128)(2,1)S(1)}, u32[]{:S(2)}, u32[]{:S(2)}) %collective-permute-start.6) | collective-permute-done | bytes 409632 | tf_op jit(solution)/shard_map/while/body/eval_jaxpr/ppermute | solution.py:18
  486.2 11.4 %collective-permute-done = bf16[160,1280]{1,0:T(8,128)(2,1)} collective-permute-done((bf16[160,1280]{1,0:T(8,128)(2,1)}, bf16[160,1280]{1,0:T(8,128)(2,1)}, u32[]{:S(2)}, u32[]{:S(2)}) %collective-permute-start) | collective-permute-done | bytes 409632 | tf_op jit(solution)/shard_map/while/body/eval_jaxpr/ppermute | solution.py:18
  500.1 10.2 %collective-permute-start.3 = (bf16[160,1280]{1,0:T(8,128)(2,1)}, bf16[160,1280]{1,0:T(8,128)(2,1)S(1)}, u32[]{:S(2)}, u32[]{:S(2)}) collective-permute-start(bf16[160,1280]{1,0:T(8,128)(2,1)} %collective-permute-done.1), channel_id=1, source_target_pairs={{0,28},{4,0},{8,4},{12,8},{16,12},{20,16},{24,20},{28,24},{1,29},{... | collective-permute-start | bytes 1228808 | tf_op jit(solution)/shard_map/while/body/eval_jaxpr/ppermute | solution.py:21
  518.8 11.9 %collective-permute-start.5 = (bf16[160,1280]{1,0:T(8,128)(2,1)S(1)}, bf16[160,1280]{1,0:T(8,128)(2,1)S(1)}, u32[]{:S(2)}, u32[]{:S(2)}) collective-permute-start(bf16[160,1280]{1,0:T(8,128)(2,1)S(1)} %collective-permute-done.3), channel_id=1, source_target_pairs={{0,28},{4,0},{8,4},{12,8},{16,12},{20,16},{24,20},{28,24},{1,29},{... | collective-permute-start | bytes 1228808 | tf_op jit(solution)/shard_map/while/body/eval_jaxpr/ppermute | solution.py:21
  538.8 8.3 %collective-permute-done.6 = bf16[160,1280]{1,0:T(8,128)(2,1)S(1)} collective-permute-done((bf16[160,1280]{1,0:T(8,128)(2,1)S(1)}, bf16[160,1280]{1,0:T(8,128)(2,1)S(1)}, u32[]{:S(2)}, u32[]{:S(2)}) %collective-permute-start.6) | collective-permute-done | bytes 409632 | tf_op jit(solution)/shard_map/while/body/eval_jaxpr/ppermute | solution.py:18
  553.8 5.1 collective-permute-start.1
  559.0 10.6 %collective-permute-done = bf16[160,1280]{1,0:T(8,128)(2,1)} collective-permute-done((bf16[160,1280]{1,0:T(8,128)(2,1)}, bf16[160,1280]{1,0:T(8,128)(2,1)}, u32[]{:S(2)}, u32[]{:S(2)}) %collective-permute-start) | collective-permute-done | bytes 409632 | tf_op jit(solution)/shard_map/while/body/eval_jaxpr/ppermute | solution.py:18
  572.1 6.9 collective-permute-start.3
  581.1 7.3 %collective-permute-done.2 = bf16[160,1280]{1,0:T(8,128)(2,1)S(1)} collective-permute-done((bf16[160,1280]{1,0:T(8,128)(2,1)}, bf16[160,1280]{1,0:T(8,128)(2,1)S(1)}, u32[]{:S(2)}, u32[]{:S(2)}) %collective-permute-start.2) | collective-permute-done | bytes 409632 | tf_op jit(solution)/shard_map/while/body/eval_jaxpr/ppermute | solution.py:18
  590.8 7.0 %collective-permute-start.5 = (bf16[160,1280]{1,0:T(8,128)(2,1)S(1)}, bf16[160,1280]{1,0:T(8,128)(2,1)S(1)}, u32[]{:S(2)}, u32[]{:S(2)}) collective-permute-start(bf16[160,1280]{1,0:T(8,128)(2,1)S(1)} %collective-permute-done.3), channel_id=1, source_target_pairs={{0,28},{4,0},{8,4},{12,8},{16,12},{20,16},{24,20},{28,24},{1,29},{... | collective-permute-start | bytes 1228808 | tf_op jit(solution)/shard_map/while/body/eval_jaxpr/ppermute | solution.py:21
  597.9 8.7 %collective-permute-done.4 = bf16[160,1280]{1,0:T(8,128)(2,1)S(1)} collective-permute-done((bf16[160,1280]{1,0:T(8,128)(2,1)S(1)}, bf16[160,1280]{1,0:T(8,128)(2,1)S(1)}, u32[]{:S(2)}, u32[]{:S(2)}) %collective-permute-start.4) | collective-permute-done | bytes 409632 | tf_op jit(solution)/shard_map/while/body/eval_jaxpr/ppermute | solution.py:18
  609.2 12.9 %collective-permute-done.6 = bf16[160,1280]{1,0:T(8,128)(2,1)S(1)} collective-permute-done((bf16[160,1280]{1,0:T(8,128)(2,1)S(1)}, bf16[160,1280]{1,0:T(8,128)(2,1)S(1)}, u32[]{:S(2)}, u32[]{:S(2)}) %collective-permute-start.6) | collective-permute-done | bytes 409632 | tf_op jit(solution)/shard_map/while/body/eval_jaxpr/ppermute | solution.py:18
  633.5 8.9 %collective-permute-done = bf16[160,1280]{1,0:T(8,128)(2,1)} collective-permute-done((bf16[160,1280]{1,0:T(8,128)(2,1)}, bf16[160,1280]{1,0:T(8,128)(2,1)}, u32[]{:S(2)}, u32[]{:S(2)}) %collective-permute-start) | collective-permute-done | bytes 409632 | tf_op jit(solution)/shard_map/while/body/eval_jaxpr/ppermute | solution.py:18
  644.9 5.5 collective-permute-start.3
  652.6 9.0 %collective-permute-done.2 = bf16[160,1280]{1,0:T(8,128)(2,1)S(1)} collective-permute-done((bf16[160,1280]{1,0:T(8,128)(2,1)}, bf16[160,1280]{1,0:T(8,128)(2,1)S(1)}, u32[]{:S(2)}, u32[]{:S(2)}) %collective-permute-start.2) | collective-permute-done | bytes 409632 | tf_op jit(solution)/shard_map/while/body/eval_jaxpr/ppermute | solution.py:18
  664.0 5.4 collective-permute-start.5
  669.5 11.1 %collective-permute-done.4 = bf16[160,1280]{1,0:T(8,128)(2,1)S(1)} collective-permute-done((bf16[160,1280]{1,0:T(8,128)(2,1)S(1)}, bf16[160,1280]{1,0:T(8,128)(2,1)S(1)}, u32[]{:S(2)}, u32[]{:S(2)}) %collective-permute-start.4) | collective-permute-done | bytes 409632 | tf_op jit(solution)/shard_map/while/body/eval_jaxpr/ppermute | solution.py:18
  683.1 10.5 %collective-permute-done.6 = bf16[160,1280]{1,0:T(8,128)(2,1)S(1)} collective-permute-done((bf16[160,1280]{1,0:T(8,128)(2,1)S(1)}, bf16[160,1280]{1,0:T(8,128)(2,1)S(1)}, u32[]{:S(2)}, u32[]{:S(2)}) %collective-permute-start.6) | collective-permute-done | bytes 409632 | tf_op jit(solution)/shard_map/while/body/eval_jaxpr/ppermute | solution.py:18
  (242 shorter events, 230.9 us)
Async XLA Ops:
  30.6 17.9 %collective-permute-start = (bf16[160,1280]{1,0:T(8,128)(2,1)}, bf16[160,1280]{1,0:T(8,128)(2,1)}, u32[]{:S(2)}, u32[]{:S(2)}) collective-permute-start(bf16[160,1280]{1,0:T(8,128)(2,1)} %get-tuple-element.211), channel_id=1, source_target_pairs={{0,4},{4,8},{8,12},{12,16},{16,20},{20,24},{24,28},{28,0},{1,5},{5... | collective-permute-start | bytes 1228808 | tf_op jit(solution)/shard_map/while/body/eval_jaxpr/ppermute | solution.py:18
  32.2 20.1 %collective-permute-start.1 = (bf16[160,1280]{1,0:T(8,128)(2,1)}, bf16[160,1280]{1,0:T(8,128)(2,1)}, u32[]{:S(2)}, u32[]{:S(2)}) collective-permute-start(bf16[160,1280]{1,0:T(8,128)(2,1)} %get-tuple-element.211), channel_id=1, source_target_pairs={{0,28},{4,0},{8,4},{12,8},{16,12},{20,16},{24,20},{28,24},{1,29},{... | collective-permute-start | bytes 1228808 | tf_op jit(solution)/shard_map/while/body/eval_jaxpr/ppermute | solution.py:21
  48.5 19.9 %collective-permute-start.2 = (bf16[160,1280]{1,0:T(8,128)(2,1)}, bf16[160,1280]{1,0:T(8,128)(2,1)S(1)}, u32[]{:S(2)}, u32[]{:S(2)}) collective-permute-start(bf16[160,1280]{1,0:T(8,128)(2,1)} %collective-permute-done), channel_id=1, source_target_pairs={{0,4},{4,8},{8,12},{12,16},{16,20},{20,24},{24,28},{28,0},{1,5},{5... | collective-permute-start | bytes 1228808 | tf_op jit(solution)/shard_map/while/body/eval_jaxpr/ppermute | solution.py:18
  52.3 20.7 %collective-permute-start.3 = (bf16[160,1280]{1,0:T(8,128)(2,1)}, bf16[160,1280]{1,0:T(8,128)(2,1)S(1)}, u32[]{:S(2)}, u32[]{:S(2)}) collective-permute-start(bf16[160,1280]{1,0:T(8,128)(2,1)} %collective-permute-done.1), channel_id=1, source_target_pairs={{0,28},{4,0},{8,4},{12,8},{16,12},{20,16},{24,20},{28,24},{1,29},{... | collective-permute-start | bytes 1228808 | tf_op jit(solution)/shard_map/while/body/eval_jaxpr/ppermute | solution.py:21
  68.4 20.7 %collective-permute-start.4 = (bf16[160,1280]{1,0:T(8,128)(2,1)S(1)}, bf16[160,1280]{1,0:T(8,128)(2,1)S(1)}, u32[]{:S(2)}, u32[]{:S(2)}) collective-permute-start(bf16[160,1280]{1,0:T(8,128)(2,1)S(1)} %collective-permute-done.2), channel_id=1, source_target_pairs={{0,4},{4,8},{8,12},{12,16},{16,20},{20,24},{24,28},{28,0},{1,5},{5... | collective-permute-start | bytes 1228808 | tf_op jit(solution)/shard_map/while/body/eval_jaxpr/ppermute | solution.py:18
  73.0 19.3 %collective-permute-start.5 = (bf16[160,1280]{1,0:T(8,128)(2,1)S(1)}, bf16[160,1280]{1,0:T(8,128)(2,1)S(1)}, u32[]{:S(2)}, u32[]{:S(2)}) collective-permute-start(bf16[160,1280]{1,0:T(8,128)(2,1)S(1)} %collective-permute-done.3), channel_id=1, source_target_pairs={{0,28},{4,0},{8,4},{12,8},{16,12},{20,16},{24,20},{28,24},{1,29},{... | collective-permute-start | bytes 1228808 | tf_op jit(solution)/shard_map/while/body/eval_jaxpr/ppermute | solution.py:21
  110.4 18.0 %collective-permute-start = (bf16[160,1280]{1,0:T(8,128)(2,1)}, bf16[160,1280]{1,0:T(8,128)(2,1)}, u32[]{:S(2)}, u32[]{:S(2)}) collective-permute-start(bf16[160,1280]{1,0:T(8,128)(2,1)} %get-tuple-element.211), channel_id=1, source_target_pairs={{0,4},{4,8},{8,12},{12,16},{16,20},{20,24},{24,28},{28,0},{1,5},{5... | collective-permute-start | bytes 1228808 | tf_op jit(solution)/shard_map/while/body/eval_jaxpr/ppermute | solution.py:18
  110.4 20.5 %collective-permute-start.1 = (bf16[160,1280]{1,0:T(8,128)(2,1)}, bf16[160,1280]{1,0:T(8,128)(2,1)}, u32[]{:S(2)}, u32[]{:S(2)}) collective-permute-start(bf16[160,1280]{1,0:T(8,128)(2,1)} %get-tuple-element.211), channel_id=1, source_target_pairs={{0,28},{4,0},{8,4},{12,8},{16,12},{20,16},{24,20},{28,24},{1,29},{... | collective-permute-start | bytes 1228808 | tf_op jit(solution)/shard_map/while/body/eval_jaxpr/ppermute | solution.py:21
  128.5 19.7 %collective-permute-start.2 = (bf16[160,1280]{1,0:T(8,128)(2,1)}, bf16[160,1280]{1,0:T(8,128)(2,1)S(1)}, u32[]{:S(2)}, u32[]{:S(2)}) collective-permute-start(bf16[160,1280]{1,0:T(8,128)(2,1)} %collective-permute-done), channel_id=1, source_target_pairs={{0,4},{4,8},{8,12},{12,16},{16,20},{20,24},{24,28},{28,0},{1,5},{5... | collective-permute-start | bytes 1228808 | tf_op jit(solution)/shard_map/while/body/eval_jaxpr/ppermute | solution.py:18
  130.9 19.6 %collective-permute-start.3 = (bf16[160,1280]{1,0:T(8,128)(2,1)}, bf16[160,1280]{1,0:T(8,128)(2,1)S(1)}, u32[]{:S(2)}, u32[]{:S(2)}) collective-permute-start(bf16[160,1280]{1,0:T(8,128)(2,1)} %collective-permute-done.1), channel_id=1, source_target_pairs={{0,28},{4,0},{8,4},{12,8},{16,12},{20,16},{24,20},{28,24},{1,29},{... | collective-permute-start | bytes 1228808 | tf_op jit(solution)/shard_map/while/body/eval_jaxpr/ppermute | solution.py:21
  148.1 19.1 %collective-permute-start.4 = (bf16[160,1280]{1,0:T(8,128)(2,1)S(1)}, bf16[160,1280]{1,0:T(8,128)(2,1)S(1)}, u32[]{:S(2)}, u32[]{:S(2)}) collective-permute-start(bf16[160,1280]{1,0:T(8,128)(2,1)S(1)} %collective-permute-done.2), channel_id=1, source_target_pairs={{0,4},{4,8},{8,12},{12,16},{16,20},{20,24},{24,28},{28,0},{1,5},{5... | collective-permute-start | bytes 1228808 | tf_op jit(solution)/shard_map/while/body/eval_jaxpr/ppermute | solution.py:18
  150.5 19.3 %collective-permute-start.5 = (bf16[160,1280]{1,0:T(8,128)(2,1)S(1)}, bf16[160,1280]{1,0:T(8,128)(2,1)S(1)}, u32[]{:S(2)}, u32[]{:S(2)}) collective-permute-start(bf16[160,1280]{1,0:T(8,128)(2,1)S(1)} %collective-permute-done.3), channel_id=1, source_target_pairs={{0,28},{4,0},{8,4},{12,8},{16,12},{20,16},{24,20},{28,24},{1,29},{... | collective-permute-start | bytes 1228808 | tf_op jit(solution)/shard_map/while/body/eval_jaxpr/ppermute | solution.py:21
  187.0 16.4 %collective-permute-start = (bf16[160,1280]{1,0:T(8,128)(2,1)}, bf16[160,1280]{1,0:T(8,128)(2,1)}, u32[]{:S(2)}, u32[]{:S(2)}) collective-permute-start(bf16[160,1280]{1,0:T(8,128)(2,1)} %get-tuple-element.211), channel_id=1, source_target_pairs={{0,4},{4,8},{8,12},{12,16},{16,20},{20,24},{24,28},{28,0},{1,5},{5... | collective-permute-start | bytes 1228808 | tf_op jit(solution)/shard_map/while/body/eval_jaxpr/ppermute | solution.py:18
  187.0 18.9 %collective-permute-start.1 = (bf16[160,1280]{1,0:T(8,128)(2,1)}, bf16[160,1280]{1,0:T(8,128)(2,1)}, u32[]{:S(2)}, u32[]{:S(2)}) collective-permute-start(bf16[160,1280]{1,0:T(8,128)(2,1)} %get-tuple-element.211), channel_id=1, source_target_pairs={{0,28},{4,0},{8,4},{12,8},{16,12},{20,16},{24,20},{28,24},{1,29},{... | collective-permute-start | bytes 1228808 | tf_op jit(solution)/shard_map/while/body/eval_jaxpr/ppermute | solution.py:21
  203.4 18.8 %collective-permute-start.2 = (bf16[160,1280]{1,0:T(8,128)(2,1)}, bf16[160,1280]{1,0:T(8,128)(2,1)S(1)}, u32[]{:S(2)}, u32[]{:S(2)}) collective-permute-start(bf16[160,1280]{1,0:T(8,128)(2,1)} %collective-permute-done), channel_id=1, source_target_pairs={{0,4},{4,8},{8,12},{12,16},{16,20},{20,24},{24,28},{28,0},{1,5},{5... | collective-permute-start | bytes 1228808 | tf_op jit(solution)/shard_map/while/body/eval_jaxpr/ppermute | solution.py:18
  205.8 18.7 %collective-permute-start.3 = (bf16[160,1280]{1,0:T(8,128)(2,1)}, bf16[160,1280]{1,0:T(8,128)(2,1)S(1)}, u32[]{:S(2)}, u32[]{:S(2)}) collective-permute-start(bf16[160,1280]{1,0:T(8,128)(2,1)} %collective-permute-done.1), channel_id=1, source_target_pairs={{0,28},{4,0},{8,4},{12,8},{16,12},{20,16},{24,20},{28,24},{1,29},{... | collective-permute-start | bytes 1228808 | tf_op jit(solution)/shard_map/while/body/eval_jaxpr/ppermute | solution.py:21
  222.2 19.1 %collective-permute-start.4 = (bf16[160,1280]{1,0:T(8,128)(2,1)S(1)}, bf16[160,1280]{1,0:T(8,128)(2,1)S(1)}, u32[]{:S(2)}, u32[]{:S(2)}) collective-permute-start(bf16[160,1280]{1,0:T(8,128)(2,1)S(1)} %collective-permute-done.2), channel_id=1, source_target_pairs={{0,4},{4,8},{8,12},{12,16},{16,20},{20,24},{24,28},{28,0},{1,5},{5... | collective-permute-start | bytes 1228808 | tf_op jit(solution)/shard_map/while/body/eval_jaxpr/ppermute | solution.py:18
  224.6 19.3 %collective-permute-start.5 = (bf16[160,1280]{1,0:T(8,128)(2,1)S(1)}, bf16[160,1280]{1,0:T(8,128)(2,1)S(1)}, u32[]{:S(2)}, u32[]{:S(2)}) collective-permute-start(bf16[160,1280]{1,0:T(8,128)(2,1)S(1)} %collective-permute-done.3), channel_id=1, source_target_pairs={{0,28},{4,0},{8,4},{12,8},{16,12},{20,16},{24,20},{28,24},{1,29},{... | collective-permute-start | bytes 1228808 | tf_op jit(solution)/shard_map/while/body/eval_jaxpr/ppermute | solution.py:21
  261.1 16.4 %collective-permute-start = (bf16[160,1280]{1,0:T(8,128)(2,1)}, bf16[160,1280]{1,0:T(8,128)(2,1)}, u32[]{:S(2)}, u32[]{:S(2)}) collective-permute-start(bf16[160,1280]{1,0:T(8,128)(2,1)} %get-tuple-element.211), channel_id=1, source_target_pairs={{0,4},{4,8},{8,12},{12,16},{16,20},{20,24},{24,28},{28,0},{1,5},{5... | collective-permute-start | bytes 1228808 | tf_op jit(solution)/shard_map/while/body/eval_jaxpr/ppermute | solution.py:18
  261.1 18.9 %collective-permute-start.1 = (bf16[160,1280]{1,0:T(8,128)(2,1)}, bf16[160,1280]{1,0:T(8,128)(2,1)}, u32[]{:S(2)}, u32[]{:S(2)}) collective-permute-start(bf16[160,1280]{1,0:T(8,128)(2,1)} %get-tuple-element.211), channel_id=1, source_target_pairs={{0,28},{4,0},{8,4},{12,8},{16,12},{20,16},{24,20},{28,24},{1,29},{... | collective-permute-start | bytes 1228808 | tf_op jit(solution)/shard_map/while/body/eval_jaxpr/ppermute | solution.py:21
  277.4 18.8 %collective-permute-start.2 = (bf16[160,1280]{1,0:T(8,128)(2,1)}, bf16[160,1280]{1,0:T(8,128)(2,1)S(1)}, u32[]{:S(2)}, u32[]{:S(2)}) collective-permute-start(bf16[160,1280]{1,0:T(8,128)(2,1)} %collective-permute-done), channel_id=1, source_target_pairs={{0,4},{4,8},{8,12},{12,16},{16,20},{20,24},{24,28},{28,0},{1,5},{5... | collective-permute-start | bytes 1228808 | tf_op jit(solution)/shard_map/while/body/eval_jaxpr/ppermute | solution.py:18
  279.9 18.7 %collective-permute-start.3 = (bf16[160,1280]{1,0:T(8,128)(2,1)}, bf16[160,1280]{1,0:T(8,128)(2,1)S(1)}, u32[]{:S(2)}, u32[]{:S(2)}) collective-permute-start(bf16[160,1280]{1,0:T(8,128)(2,1)} %collective-permute-done.1), channel_id=1, source_target_pairs={{0,28},{4,0},{8,4},{12,8},{16,12},{20,16},{24,20},{28,24},{1,29},{... | collective-permute-start | bytes 1228808 | tf_op jit(solution)/shard_map/while/body/eval_jaxpr/ppermute | solution.py:21
  296.3 19.1 %collective-permute-start.4 = (bf16[160,1280]{1,0:T(8,128)(2,1)S(1)}, bf16[160,1280]{1,0:T(8,128)(2,1)S(1)}, u32[]{:S(2)}, u32[]{:S(2)}) collective-permute-start(bf16[160,1280]{1,0:T(8,128)(2,1)S(1)} %collective-permute-done.2), channel_id=1, source_target_pairs={{0,4},{4,8},{8,12},{12,16},{16,20},{20,24},{24,28},{28,0},{1,5},{5... | collective-permute-start | bytes 1228808 | tf_op jit(solution)/shard_map/while/body/eval_jaxpr/ppermute | solution.py:18
  298.6 19.2 %collective-permute-start.5 = (bf16[160,1280]{1,0:T(8,128)(2,1)S(1)}, bf16[160,1280]{1,0:T(8,128)(2,1)S(1)}, u32[]{:S(2)}, u32[]{:S(2)}) collective-permute-start(bf16[160,1280]{1,0:T(8,128)(2,1)S(1)} %collective-permute-done.3), channel_id=1, source_target_pairs={{0,28},{4,0},{8,4},{12,8},{16,12},{20,16},{24,20},{28,24},{1,29},{... | collective-permute-start | bytes 1228808 | tf_op jit(solution)/shard_map/while/body/eval_jaxpr/ppermute | solution.py:21
  335.1 18.4 %collective-permute-start.1 = (bf16[160,1280]{1,0:T(8,128)(2,1)}, bf16[160,1280]{1,0:T(8,128)(2,1)}, u32[]{:S(2)}, u32[]{:S(2)}) collective-permute-start(bf16[160,1280]{1,0:T(8,128)(2,1)} %get-tuple-element.211), channel_id=1, source_target_pairs={{0,28},{4,0},{8,4},{12,8},{16,12},{20,16},{24,20},{28,24},{1,29},{... | collective-permute-start | bytes 1228808 | tf_op jit(solution)/shard_map/while/body/eval_jaxpr/ppermute | solution.py:21
  351.0 18.3 %collective-permute-start.2 = (bf16[160,1280]{1,0:T(8,128)(2,1)}, bf16[160,1280]{1,0:T(8,128)(2,1)S(1)}, u32[]{:S(2)}, u32[]{:S(2)}) collective-permute-start(bf16[160,1280]{1,0:T(8,128)(2,1)} %collective-permute-done), channel_id=1, source_target_pairs={{0,4},{4,8},{8,12},{12,16},{16,20},{20,24},{24,28},{28,0},{1,5},{5... | collective-permute-start | bytes 1228808 | tf_op jit(solution)/shard_map/while/body/eval_jaxpr/ppermute | solution.py:18
  353.5 18.2 %collective-permute-start.3 = (bf16[160,1280]{1,0:T(8,128)(2,1)}, bf16[160,1280]{1,0:T(8,128)(2,1)S(1)}, u32[]{:S(2)}, u32[]{:S(2)}) collective-permute-start(bf16[160,1280]{1,0:T(8,128)(2,1)} %collective-permute-done.1), channel_id=1, source_target_pairs={{0,28},{4,0},{8,4},{12,8},{16,12},{20,16},{24,20},{28,24},{1,29},{... | collective-permute-start | bytes 1228808 | tf_op jit(solution)/shard_map/while/body/eval_jaxpr/ppermute | solution.py:21
  369.3 19.1 %collective-permute-start.4 = (bf16[160,1280]{1,0:T(8,128)(2,1)S(1)}, bf16[160,1280]{1,0:T(8,128)(2,1)S(1)}, u32[]{:S(2)}, u32[]{:S(2)}) collective-permute-start(bf16[160,1280]{1,0:T(8,128)(2,1)S(1)} %collective-permute-done.2), channel_id=1, source_target_pairs={{0,4},{4,8},{8,12},{12,16},{16,20},{20,24},{24,28},{28,0},{1,5},{5... | collective-permute-start | bytes 1228808 | tf_op jit(solution)/shard_map/while/body/eval_jaxpr/ppermute | solution.py:18
  371.7 19.3 %collective-permute-start.5 = (bf16[160,1280]{1,0:T(8,128)(2,1)S(1)}, bf16[160,1280]{1,0:T(8,128)(2,1)S(1)}, u32[]{:S(2)}, u32[]{:S(2)}) collective-permute-start(bf16[160,1280]{1,0:T(8,128)(2,1)S(1)} %collective-permute-done.3), channel_id=1, source_target_pairs={{0,28},{4,0},{8,4},{12,8},{16,12},{20,16},{24,20},{28,24},{1,29},{... | collective-permute-start | bytes 1228808 | tf_op jit(solution)/shard_map/while/body/eval_jaxpr/ppermute | solution.py:21
  408.1 18.8 %collective-permute-start.1 = (bf16[160,1280]{1,0:T(8,128)(2,1)}, bf16[160,1280]{1,0:T(8,128)(2,1)}, u32[]{:S(2)}, u32[]{:S(2)}) collective-permute-start(bf16[160,1280]{1,0:T(8,128)(2,1)} %get-tuple-element.211), channel_id=1, source_target_pairs={{0,28},{4,0},{8,4},{12,8},{16,12},{20,16},{24,20},{28,24},{1,29},{... | collective-permute-start | bytes 1228808 | tf_op jit(solution)/shard_map/while/body/eval_jaxpr/ppermute | solution.py:21
  424.4 19.0 %collective-permute-start.2 = (bf16[160,1280]{1,0:T(8,128)(2,1)}, bf16[160,1280]{1,0:T(8,128)(2,1)S(1)}, u32[]{:S(2)}, u32[]{:S(2)}) collective-permute-start(bf16[160,1280]{1,0:T(8,128)(2,1)} %collective-permute-done), channel_id=1, source_target_pairs={{0,4},{4,8},{8,12},{12,16},{16,20},{20,24},{24,28},{28,0},{1,5},{5... | collective-permute-start | bytes 1228808 | tf_op jit(solution)/shard_map/while/body/eval_jaxpr/ppermute | solution.py:18
  426.9 18.9 %collective-permute-start.3 = (bf16[160,1280]{1,0:T(8,128)(2,1)}, bf16[160,1280]{1,0:T(8,128)(2,1)S(1)}, u32[]{:S(2)}, u32[]{:S(2)}) collective-permute-start(bf16[160,1280]{1,0:T(8,128)(2,1)} %collective-permute-done.1), channel_id=1, source_target_pairs={{0,28},{4,0},{8,4},{12,8},{16,12},{20,16},{24,20},{28,24},{1,29},{... | collective-permute-start | bytes 1228808 | tf_op jit(solution)/shard_map/while/body/eval_jaxpr/ppermute | solution.py:21
  443.4 18.6 %collective-permute-start.4 = (bf16[160,1280]{1,0:T(8,128)(2,1)S(1)}, bf16[160,1280]{1,0:T(8,128)(2,1)S(1)}, u32[]{:S(2)}, u32[]{:S(2)}) collective-permute-start(bf16[160,1280]{1,0:T(8,128)(2,1)S(1)} %collective-permute-done.2), channel_id=1, source_target_pairs={{0,4},{4,8},{8,12},{12,16},{16,20},{20,24},{24,28},{28,0},{1,5},{5... | collective-permute-start | bytes 1228808 | tf_op jit(solution)/shard_map/while/body/eval_jaxpr/ppermute | solution.py:18
  445.8 19.0 %collective-permute-start.5 = (bf16[160,1280]{1,0:T(8,128)(2,1)S(1)}, bf16[160,1280]{1,0:T(8,128)(2,1)S(1)}, u32[]{:S(2)}, u32[]{:S(2)}) collective-permute-start(bf16[160,1280]{1,0:T(8,128)(2,1)S(1)} %collective-permute-done.3), channel_id=1, source_target_pairs={{0,28},{4,0},{8,4},{12,8},{16,12},{20,16},{24,20},{28,24},{1,29},{... | collective-permute-start | bytes 1228808 | tf_op jit(solution)/shard_map/while/body/eval_jaxpr/ppermute | solution.py:21
  481.5 18.6 %collective-permute-start.1 = (bf16[160,1280]{1,0:T(8,128)(2,1)}, bf16[160,1280]{1,0:T(8,128)(2,1)}, u32[]{:S(2)}, u32[]{:S(2)}) collective-permute-start(bf16[160,1280]{1,0:T(8,128)(2,1)} %get-tuple-element.211), channel_id=1, source_target_pairs={{0,28},{4,0},{8,4},{12,8},{16,12},{20,16},{24,20},{28,24},{1,29},{... | collective-permute-start | bytes 1228808 | tf_op jit(solution)/shard_map/while/body/eval_jaxpr/ppermute | solution.py:21
  497.6 18.8 %collective-permute-start.2 = (bf16[160,1280]{1,0:T(8,128)(2,1)}, bf16[160,1280]{1,0:T(8,128)(2,1)S(1)}, u32[]{:S(2)}, u32[]{:S(2)}) collective-permute-start(bf16[160,1280]{1,0:T(8,128)(2,1)} %collective-permute-done), channel_id=1, source_target_pairs={{0,4},{4,8},{8,12},{12,16},{16,20},{20,24},{24,28},{28,0},{1,5},{5... | collective-permute-start | bytes 1228808 | tf_op jit(solution)/shard_map/while/body/eval_jaxpr/ppermute | solution.py:18
  500.1 18.7 %collective-permute-start.3 = (bf16[160,1280]{1,0:T(8,128)(2,1)}, bf16[160,1280]{1,0:T(8,128)(2,1)S(1)}, u32[]{:S(2)}, u32[]{:S(2)}) collective-permute-start(bf16[160,1280]{1,0:T(8,128)(2,1)} %collective-permute-done.1), channel_id=1, source_target_pairs={{0,28},{4,0},{8,4},{12,8},{16,12},{20,16},{24,20},{28,24},{1,29},{... | collective-permute-start | bytes 1228808 | tf_op jit(solution)/shard_map/while/body/eval_jaxpr/ppermute | solution.py:21
  516.4 18.2 %collective-permute-start.4 = (bf16[160,1280]{1,0:T(8,128)(2,1)S(1)}, bf16[160,1280]{1,0:T(8,128)(2,1)S(1)}, u32[]{:S(2)}, u32[]{:S(2)}) collective-permute-start(bf16[160,1280]{1,0:T(8,128)(2,1)S(1)} %collective-permute-done.2), channel_id=1, source_target_pairs={{0,4},{4,8},{8,12},{12,16},{16,20},{20,24},{24,28},{28,0},{1,5},{5... | collective-permute-start | bytes 1228808 | tf_op jit(solution)/shard_map/while/body/eval_jaxpr/ppermute | solution.py:18
  518.8 20.0 %collective-permute-start.5 = (bf16[160,1280]{1,0:T(8,128)(2,1)S(1)}, bf16[160,1280]{1,0:T(8,128)(2,1)S(1)}, u32[]{:S(2)}, u32[]{:S(2)}) collective-permute-start(bf16[160,1280]{1,0:T(8,128)(2,1)S(1)} %collective-permute-done.3), channel_id=1, source_target_pairs={{0,28},{4,0},{8,4},{12,8},{16,12},{20,16},{24,20},{28,24},{1,29},{... | collective-permute-start | bytes 1228808 | tf_op jit(solution)/shard_map/while/body/eval_jaxpr/ppermute | solution.py:21
  553.8 18.2 %collective-permute-start.1 = (bf16[160,1280]{1,0:T(8,128)(2,1)}, bf16[160,1280]{1,0:T(8,128)(2,1)}, u32[]{:S(2)}, u32[]{:S(2)}) collective-permute-start(bf16[160,1280]{1,0:T(8,128)(2,1)} %get-tuple-element.211), channel_id=1, source_target_pairs={{0,28},{4,0},{8,4},{12,8},{16,12},{20,16},{24,20},{28,24},{1,29},{... | collective-permute-start | bytes 1228808 | tf_op jit(solution)/shard_map/while/body/eval_jaxpr/ppermute | solution.py:21
  569.6 18.8 %collective-permute-start.2 = (bf16[160,1280]{1,0:T(8,128)(2,1)}, bf16[160,1280]{1,0:T(8,128)(2,1)S(1)}, u32[]{:S(2)}, u32[]{:S(2)}) collective-permute-start(bf16[160,1280]{1,0:T(8,128)(2,1)} %collective-permute-done), channel_id=1, source_target_pairs={{0,4},{4,8},{8,12},{12,16},{16,20},{20,24},{24,28},{28,0},{1,5},{5... | collective-permute-start | bytes 1228808 | tf_op jit(solution)/shard_map/while/body/eval_jaxpr/ppermute | solution.py:18
  572.1 18.7 %collective-permute-start.3 = (bf16[160,1280]{1,0:T(8,128)(2,1)}, bf16[160,1280]{1,0:T(8,128)(2,1)S(1)}, u32[]{:S(2)}, u32[]{:S(2)}) collective-permute-start(bf16[160,1280]{1,0:T(8,128)(2,1)} %collective-permute-done.1), channel_id=1, source_target_pairs={{0,28},{4,0},{8,4},{12,8},{16,12},{20,16},{24,20},{28,24},{1,29},{... | collective-permute-start | bytes 1228808 | tf_op jit(solution)/shard_map/while/body/eval_jaxpr/ppermute | solution.py:21
  588.4 18.2 %collective-permute-start.4 = (bf16[160,1280]{1,0:T(8,128)(2,1)S(1)}, bf16[160,1280]{1,0:T(8,128)(2,1)S(1)}, u32[]{:S(2)}, u32[]{:S(2)}) collective-permute-start(bf16[160,1280]{1,0:T(8,128)(2,1)S(1)} %collective-permute-done.2), channel_id=1, source_target_pairs={{0,4},{4,8},{8,12},{12,16},{16,20},{20,24},{24,28},{28,0},{1,5},{5... | collective-permute-start | bytes 1228808 | tf_op jit(solution)/shard_map/while/body/eval_jaxpr/ppermute | solution.py:18
  590.8 18.4 %collective-permute-start.5 = (bf16[160,1280]{1,0:T(8,128)(2,1)S(1)}, bf16[160,1280]{1,0:T(8,128)(2,1)S(1)}, u32[]{:S(2)}, u32[]{:S(2)}) collective-permute-start(bf16[160,1280]{1,0:T(8,128)(2,1)S(1)} %collective-permute-done.3), channel_id=1, source_target_pairs={{0,28},{4,0},{8,4},{12,8},{16,12},{20,16},{24,20},{28,24},{1,29},{... | collective-permute-start | bytes 1228808 | tf_op jit(solution)/shard_map/while/body/eval_jaxpr/ppermute | solution.py:21
  642.4 19.2 %collective-permute-start.2 = (bf16[160,1280]{1,0:T(8,128)(2,1)}, bf16[160,1280]{1,0:T(8,128)(2,1)S(1)}, u32[]{:S(2)}, u32[]{:S(2)}) collective-permute-start(bf16[160,1280]{1,0:T(8,128)(2,1)} %collective-permute-done), channel_id=1, source_target_pairs={{0,4},{4,8},{8,12},{12,16},{16,20},{20,24},{24,28},{28,0},{1,5},{5... | collective-permute-start | bytes 1228808 | tf_op jit(solution)/shard_map/while/body/eval_jaxpr/ppermute | solution.py:18
  644.9 19.1 %collective-permute-start.3 = (bf16[160,1280]{1,0:T(8,128)(2,1)}, bf16[160,1280]{1,0:T(8,128)(2,1)S(1)}, u32[]{:S(2)}, u32[]{:S(2)}) collective-permute-start(bf16[160,1280]{1,0:T(8,128)(2,1)} %collective-permute-done.1), channel_id=1, source_target_pairs={{0,28},{4,0},{8,4},{12,8},{16,12},{20,16},{24,20},{28,24},{1,29},{... | collective-permute-start | bytes 1228808 | tf_op jit(solution)/shard_map/while/body/eval_jaxpr/ppermute | solution.py:21
  661.6 19.0 %collective-permute-start.4 = (bf16[160,1280]{1,0:T(8,128)(2,1)S(1)}, bf16[160,1280]{1,0:T(8,128)(2,1)S(1)}, u32[]{:S(2)}, u32[]{:S(2)}) collective-permute-start(bf16[160,1280]{1,0:T(8,128)(2,1)S(1)} %collective-permute-done.2), channel_id=1, source_target_pairs={{0,4},{4,8},{8,12},{12,16},{16,20},{20,24},{24,28},{28,0},{1,5},{5... | collective-permute-start | bytes 1228808 | tf_op jit(solution)/shard_map/while/body/eval_jaxpr/ppermute | solution.py:18
  664.0 19.1 %collective-permute-start.5 = (bf16[160,1280]{1,0:T(8,128)(2,1)S(1)}, bf16[160,1280]{1,0:T(8,128)(2,1)S(1)}, u32[]{:S(2)}, u32[]{:S(2)}) collective-permute-start(bf16[160,1280]{1,0:T(8,128)(2,1)S(1)} %collective-permute-done.3), channel_id=1, source_target_pairs={{0,28},{4,0},{8,4},{12,8},{16,12},{20,16},{24,20},{28,24},{1,29},{... | collective-permute-start | bytes 1228808 | tf_op jit(solution)/shard_map/while/body/eval_jaxpr/ppermute | solution.py:21
  (39 other events, 1351.9 us)
